TPU v7x, 512 devices: a whole 4x8x8 slice. The times are simulated.
512 devices in a mesh: tm: 16 (over y, core), vert: 32 (over x, z).
Axes of the slice: x: 4, y: 8, z: 8, core: 2. Of those that a mesh axis runs over, the one named last changes fastest.
Arguments:
- features: bfloat16 [16, 16384, 1024], P('tm', 'vert'), may hold values from -6 to 6
- graph_weight: bfloat16 [1024, 1024], P('vert'), may hold values from -0.1875 to 0.1875
- head_weight: bfloat16 [16, 192, 1024], P('tm'), may hold values from -16 to 16
- send_rows: int32 [16, 32, 32, 16], P('tm', 'vert'), may hold values from 0 to 511, as said below
- send_count: int32 [16, 32, 32], P('tm', 'vert'), may hold values from 0 to 16, as said below
- block_index: int32 [16, 128, 3], P('tm', 'vert'), may hold values from 0 to 7, as said below
- block_values: bfloat16 [16, 16384, 3, 128], P('tm', 'vert'), may hold values from -0.3125 to 0.3125
Outputs:
- combined: bfloat16 [16, 16384, 1024], P('tm', 'vert')
Inputs may be any that keep to these rules, and one draw needn't show every extreme that they name: send_rows[s, p, q] holds 16 distinct local rows of partition p; slots from send_count[s, p, q] on are ignored. send_count[s, p, p] is 0; in every snapshot some pairs reach 16. `block_index`: the 3 entries of a block row are distinct; column blocks below 4 are the partition's own rows, the others its boundary rows in the order of columns.
All inputs are finite; a program needn't handle non-finite values.
Results may differ from a plain program's by a relative error of at most 0.0075.
Values may be sent and summed in bfloat16 or wider, within the bound.
A program may use at most 64 MiB of HBM per device.

v0:
```python
import jax
import jax.numpy as jnp
from jax import lax
from jax.sharding import PartitionSpec as P


def attend_heads(regrouped, head_piece):
    head_size = head_piece.shape[1] // 3
    count_heads = head_piece.shape[0]
    snapshots = regrouped.shape[0]
    packed = jnp.einsum("tvd,hcd->tvhc", regrouped, head_piece, preferred_element_type=jnp.float32)
    queries = packed[..., :head_size].astype(jnp.bfloat16)
    keys_part = packed[..., head_size : 2 * head_size].astype(jnp.bfloat16)
    values = packed[..., 2 * head_size :].astype(jnp.bfloat16)
    scores = jnp.einsum(
        "tvhc,svhc->vhts", queries, keys_part, preferred_element_type=jnp.float32
    ) * head_size ** (-0.5)
    causal = jnp.arange(snapshots)[:, None] >= jnp.arange(snapshots)[None, :]
    scores = jnp.where(causal, scores, -1e30)
    row_max = jnp.max(scores, axis=-1, keepdims=True)
    exponent = jnp.where(causal, jnp.exp(scores - row_max), 0.0)
    attention = (exponent / jnp.sum(exponent, axis=-1, keepdims=True)).astype(jnp.bfloat16)
    attended = jnp.einsum("vhts,svhc->tvhc", attention, values, preferred_element_type=jnp.float32)
    return attended.astype(jnp.bfloat16).reshape(
        snapshots, regrouped.shape[1], count_heads * head_size
    )


def fold_rows(left, piece):
    return jnp.dot(left, piece, preferred_element_type=jnp.float32)


def shards(features, graph_weight, head_weight, send_rows, send_count, block_index, block_values):
    inputs = features[0]
    feature_width = inputs.shape[1]
    own_count = inputs.shape[0]
    rows_list = send_rows[0, 0]
    sources = rows_list.shape[0]
    most_rows = rows_list.shape[1]
    live_slots = jnp.arange(most_rows)[None, :] < send_count[0, 0][:, None]
    projected = fold_rows(inputs, lax.all_gather(graph_weight, "vert", axis=0, tiled=True)).astype(
        jnp.bfloat16
    )
    picked = jnp.take(projected, rows_list.reshape(-1), axis=0).reshape(
        sources, most_rows, feature_width
    )
    picked = jnp.where(live_slots[:, :, None], picked, jnp.zeros_like(picked))
    received = lax.all_to_all(picked, "vert", split_axis=0, concat_axis=0, tiled=True)
    block_size = block_values.shape[-1]
    index_list = block_index[0]
    own_blocks = index_list.shape[0]
    chosen_count = index_list.shape[1]
    columns = jnp.concatenate(
        [projected, received.reshape(sources * most_rows, feature_width)], axis=0
    )
    columns = columns.reshape(-1, block_size, feature_width)
    chosen = jnp.take(columns, index_list.reshape(-1), axis=0).reshape(
        own_blocks, chosen_count, block_size, feature_width
    )
    edge_weights = block_values[0].reshape(own_blocks, block_size, chosen_count, block_size)
    summed = jnp.einsum("rikj,rkjd->rid", edge_weights, chosen, preferred_element_type=jnp.float32)
    pre_act = projected.astype(jnp.float32) + summed.reshape(own_count, feature_width)
    hidden = jax.nn.relu(pre_act).astype(jnp.bfloat16)
    regrouped = lax.all_to_all(hidden[None], "tm", split_axis=1, concat_axis=0, tiled=True)
    attended = attend_heads(regrouped, lax.all_gather(head_weight, "tm", axis=0, tiled=True))
    returned = lax.all_to_all(attended, "tm", split_axis=0, concat_axis=1, tiled=True)
    combined = (hidden.astype(jnp.float32) + returned[0].astype(jnp.float32)).astype(jnp.bfloat16)
    return combined[None]


def solution(mesh):
    return jax.shard_map(
        shards,
        mesh=mesh,
        in_specs=(
            P("tm", "vert", None),
            P("vert", None),
            P("tm", None, None),
            P("tm", "vert", None, None),
            P("tm", "vert", None),
            P("tm", "vert", None),
            P("tm", "vert", None, None),
        ),
        out_specs=P("tm", "vert", None),
        check_vma=False,
    )
```

profile of v0, /device:TPU:1, one launch (start us, length us, event | category | flops | bytes accessed | tf_op | source)
XLA Modules:
  0.0 263.2 jit_solution(4501448001142894589)
XLA Ops:
  6.5 0.0 copy-start
  6.5 0.0 all-gather.3.cloned.1.call-start
  6.5 0.7 all-gather.3.cloned.1.call-update
  7.3 0.0 all-gather.5.cloned.1.call-start
  7.3 0.7 all-gather.5.cloned.1.call-update
  8.0 0.8 copy.39
  8.8 0.1 reshape_squeeze.15
  8.9 0.7 compare_and_fusion
  9.6 0.1 copy.38
  9.7 0.7 iota_compare_fusion
  10.4 84.7 %all-gather.3.cloned.1.call-done = bf16[1024,1024]{1,0:T(8,128)(2,1)} async-done(((bf16[32,1024]{1,0:T(8,128)(2,1)}), bf16[1024,1024]{1,0:T(8,128)(2,1)}) %all-gather.3.cloned.1.call-update) | async-done | bytes 2097168 | tf_op jit(solution)/shard_map/all_gather | solution.py:41
  95.1 0.0 copy-done
  95.1 2.8 %convolution_convert_fusion = bf16[512,1024]{1,0:T(8,128)(2,1)S(1)} fusion(bf16[1024,1024]{1,0:T(8,128)(2,1)} %all-gather.3.cloned.1.call-done, bf16[1,512,1024]{2,1,0:T(8,128)(2,1)S(1)} %copy-done), kind=kOutput, calls=%fused_computation.30 | convolution fusion | flops 1074266112 | bytes 4194304 | tf_op jit(solution)/shard_map/dot_general | solution.py:30
  97.9 2.1 gather_fusion
  100.0 0.0 copy-start.1
  100.0 1.2 select_select_fusion
  101.2 5.9 %all-to-all-start = ((bf16[32,16,1024]{2,1,0:T(8,128)(2,1)}), bf16[32,16,1024]{2,1,0:T(8,128)(2,1)S(1)}, u32[]{:S(2)}, u32[]{:S(2)}) async-start(bf16[32,16,1024]{2,1,0:T(8,128)(2,1)} %select_select_fusion), calls=%async_computation | async-start | bytes 2097152 | tf_op jit(solution)/shard_map/all_to_all | solution.py:48
  107.1 0.0 copy-done.1
  107.2 0.1 copy.37
  107.2 0.1 reshape_squeeze.16
  107.4 19.0 %all-to-all-done = bf16[32,16,1024]{2,1,0:T(8,128)(2,1)S(1)} async-done(((bf16[32,16,1024]{2,1,0:T(8,128)(2,1)}), bf16[32,16,1024]{2,1,0:T(8,128)(2,1)S(1)}, u32[]{:S(2)}, u32[]{:S(2)}) %all-to-all-start) | async-done | bytes 1048608 | tf_op jit(solution)/shard_map/all_to_all | solution.py:48
  126.4 1.5 pad_maximum_fusion
  127.9 0.0 copy-start.2
  127.9 4.2 %gather_fusion.1 = bf16[12,128,1024]{2,1,0:T(8,128)(2,1)} fusion(bf16[8,128,1024]{2,1,0:T(8,128)(2,1)} %bitcast.57, s32[1024]{0:T(1024)S(1)} %pad_clamp_fusion), kind=kCustom, calls=%fused_computation.1 | custom fusion | bytes 6291504 | tf_op jit(solution)/shard_map/jit(_take)/gather | solution.py:57
  132.1 0.0 copy-done.2
  132.1 2.8 %fusion.4 = f32[4,1024,128,1]{1,2,3,0:T(8,128)S(1)} fusion(bf16[4,3,128,1024]{3,2,1,0:T(8,128)(2,1)} %bitcast.63, pred[4,3]{1,0:T(4,128)(4,1)S(1)} %compare_and_fusion.1, bf16[4,128,3,128]{3,1,0,2:T(8,128)(2,1)S(1)} %bitcast.67), kind=kOutput, calls=%fused_computation.9 | convolution fusion | flops 404226048 | bytes 5636108 | tf_op jit(solution)/shard_map/rikj,rkjd->rid/dot_general | solution.py:61
  134.9 0.4 fusion.13
  135.3 3.0 %copy.63 = bf16[1,512,1024]{2,0,1:T(2,128)(2,1)} copy(bf16[1,512,1024]{2,1,0:T(8,128)(2,1)S(1)} %bitcast.58) | data formatting | bytes 2097152 | tf_op jit(solution)/shard_map/broadcast_in_dim | solution.py:64
  138.3 0.5 broadcast.92
  138.8 8.1 %reduce = bf16[512,1024]{1,0:T(8,128)(2,1)S(1)} reduce(bf16[512,1,1024]{2,1,0:T(2,128)(2,1)} %bitcast.60, bf16[]{:T(256)} %broadcast.92), dimensions={1}, to_apply=%bitcast.56.reduce_sub_computation | reduce | bytes 2097154
  146.9 1.6 reshape.151
  148.5 16.7 %all-to-all-start.1 = ((bf16[16,2,16384]{2,1,0:T(2,128)(2,1)}), bf16[16,2,16384]{2,1,0:T(2,128)(2,1)S(1)}, u32[]{:S(2)}, u32[]{:S(2)}) async-start(bf16[16,2,16384]{2,1,0:T(2,128)(2,1)} %reshape.151), calls=%async_computation.1 | async-start | bytes 2097152 | tf_op jit(solution)/shard_map/all_to_all | solution.py:64
  165.2 28.0 %all-to-all-done.1 = bf16[16,2,16384]{2,1,0:T(2,128)(2,1)S(1)} async-done(((bf16[16,2,16384]{2,1,0:T(2,128)(2,1)}), bf16[16,2,16384]{2,1,0:T(2,128)(2,1)S(1)}, u32[]{:S(2)}, u32[]{:S(2)}) %all-to-all-start.1) | async-done | bytes 1048608 | tf_op jit(solution)/shard_map/all_to_all | solution.py:64
  193.2 3.5 %reshape.152 = bf16[512,1,1024]{2,1,0:T(2,128)(2,1)} reshape(bf16[16,2,16384]{2,1,0:T(2,128)(2,1)S(1)} %all-to-all-done.1) | data formatting | bytes 2097152
  196.7 2.0 copy.51
  198.7 0.0 all-gather.5.cloned.1.call-done
  198.7 7.5 %fusion.7 = bf16[16,32,16,192]{3,1,2,0:T(8,128)(2,1)S(1)} fusion(bf16[16,32,1024,1]{2,1,3,0:T(8,128)(2,1)S(1)} %bitcast.64, bf16[16,192,1024]{2,1,0:T(8,128)(2,1)} %all-gather.5.cloned.1.call-done), kind=kOutput, calls=%fused_computation.12 | convolution fusion | flops 3222798336 | bytes 10485760 | tf_op jit(solution)/shard_map/tvd,hcd->tvhc/dot_general | solution.py:11
  206.3 1.8 fusion.32
  208.1 4.7 %fusion.15 = f32[32,16,16,16]{2,3,1,0:T(8,128)S(1)} fusion(bf16[16,32,16,64]{3,1,2,0:T(8,128)(2,1)S(1)} %get-tuple-element.6, bf16[16,32,16,64]{3,1,2,0:T(8,128)(2,1)S(1)} %get-tuple-element.7), kind=kOutput, calls=%fused_computation.21 | convolution fusion | flops 16777216 | bytes 2621440 | tf_op jit(solution)/shard_map/tvhc,svhc->vhts/dot_general | solution.py:15
  212.7 2.1 fusion.33
  214.8 3.2 %convert_bitcast_fusion = bf16[16,32,16,64]{3,0,2,1:T(8,128)(2,1)S(1)} fusion(f32[32,16,16,16]{2,3,1,0:T(8,128)S(1)} %get-tuple-element.9, f32[32,16,16]{2,1,0:T(8,128)S(1)} %get-tuple-element.8, bf16[16,32,16,64]{3,1,2,0:T(8,128)(2,1)S(1)} %get-tuple-element.5), kind=kOutput, calls=%fused_computation.24 | convolution fusion | flops 17563648 | bytes 2654208 | tf_op jit(solution)/shard_map/vhts,svhc->tvhc/dot_general | solution.py:23
  218.1 1.9 copy.47
  220.0 3.2 %reshape.129 = bf16[16,32,1024]{2,1,0:T(8,128)(2,1)S(1)} reshape(bf16[16,32,16,64]{3,2,1,0:T(8,128)(2,1)} %copy.47) | data formatting | bytes 2097152 | tf_op jit(solution)/shard_map/reshape | solution.py:24
  223.2 31.7 %all_to_all.26 = bf16[16,32,1024]{2,1,0:T(8,128)(2,1)S(1)} all-to-all(bf16[16,32,1024]{2,1,0:T(8,128)(2,1)S(1)} %reshape.129), channel_id=1, replica_groups=mesh['tm'=16,'vert'=32] {'tm'}, dimensions={0} | all-to-all | bytes 2097152 | tf_op jit(solution)/shard_map/all_to_all | solution.py:66
  254.9 1.4 fusion.25
  (6 shorter events, 0.0 us)
Async XLA Ops:
  6.5 88.6 %copy-start = (bf16[1,512,1024]{2,1,0:T(8,128)(2,1)S(1)}, bf16[1,512,1024]{2,1,0:T(8,128)(2,1)}, u32[]{:S(2)}) copy-start(bf16[1,512,1024]{2,1,0:T(8,128)(2,1)} %param.7) | copy-start | bytes 3145732
  6.5 88.5 %all-gather.3.cloned.1.call-start = ((), (), s32[]{:S(2)}) async-start(), calls=%async_computation.3 | async-start | bytes 2162688 | tf_op jit(solution)/shard_map/all_gather | solution.py:41
  7.3 191.5 %all-gather.5.cloned.1.call-start = ((), (), s32[]{:S(2)}) async-start(), calls=%async_computation.4 | async-start | bytes 6684672 | tf_op jit(solution)/shard_map/all_gather | solution.py:65
  100.0 7.1 %copy-start.1 = (s32[1,4,3]{1,0,2:T(1,128)S(1)}, s32[1,4,3]{1,0,2:T(1,128)}, u32[]{:S(2)}) copy-start(s32[1,4,3]{1,0,2:T(1,128)} %param.12) | copy-start | bytes 148
  101.2 25.2 %all-to-all-start = ((bf16[32,16,1024]{2,1,0:T(8,128)(2,1)}), bf16[32,16,1024]{2,1,0:T(8,128)(2,1)S(1)}, u32[]{:S(2)}, u32[]{:S(2)}) async-start(bf16[32,16,1024]{2,1,0:T(8,128)(2,1)} %select_select_fusion), calls=%async_computation | async-start | bytes 2097152 | tf_op jit(solution)/shard_map/all_to_all | solution.py:48
  127.9 4.2 %copy-start.2 = (bf16[1,512,3,128]{3,1,2,0:T(8,128)(2,1)S(1)}, bf16[1,512,3,128]{3,1,2,0:T(8,128)(2,1)}, u32[]{:S(2)}) copy-start(bf16[1,512,3,128]{3,1,2,0:T(8,128)(2,1)} %param.13) | copy-start | bytes 1179652
  148.5 44.7 %all-to-all-start.1 = ((bf16[16,2,16384]{2,1,0:T(2,128)(2,1)}), bf16[16,2,16384]{2,1,0:T(2,128)(2,1)S(1)}, u32[]{:S(2)}, u32[]{:S(2)}) async-start(bf16[16,2,16384]{2,1,0:T(2,128)(2,1)} %reshape.151), calls=%async_computation.1 | async-start | bytes 2097152 | tf_op jit(solution)/shard_map/all_to_all | solution.py:64
Sparse Core Ops, SparseCore 0:
  10.5 84.5 all-gather.2
  97.2 50.5 all-gather.4
where the time goes:
time: 264 us; the launch traced here: 263 us
  waiting for transfers between devices  133 us (50%)
  blocking collectives  31.7 us (12%)
  local copies, waits for them, and re-layouts  24.9 us (9%)
  starting transfers between devices  22.7 us (9%)
  matrix products  21 us (8%)
  other arithmetic  16.2 us (6%)
  between operations  13.5 us (5%)
    all_gather x1, waiting for transfers between devices, shards(): lax.all_gather(graph_weight, 'vert', axis=0, tiled=True)  84.7 us
    all_to_all x1, blocking collectives, shards(): lax.all_to_all(attended, 'tm', split_axis=0, concat_axis=1, tiled=True)  31.7 us
    all_to_all x1, waiting for transfers between devices, shards(): lax.all_to_all(hidden[None], 'tm', split_axis=1, concat_axis=0, tiled=True)  28 us
    all_to_all x1, waiting for transfers between devices, shards(): lax.all_to_all(picked, 'vert', split_axis=0, concat_axis=0, tiled=True)  19 us
    all_to_all x1, starting transfers between devices, shards(): lax.all_to_all(hidden[None], 'tm', split_axis=1, concat_axis=0, tiled=True)  16.7 us
    unnamed x12, local copies, waits for them, and re-layouts  8.44 us
    unnamed x1, other arithmetic  8.09 us
    dot_general x1, matrix products, attend_heads(): jnp.einsum('tvd,hcd->tvhc', regrouped, head_piece, preferred_element_type...  7.53 us
  transfers between devices with their start and end apart: 4, of which 3 were waited for; matrix products, arithmetic and copies ran while one was open for 14% of the time, Pallas kernels for 0%

commit v1 on v0

v1 whole, which is shorter than its diff:
```python
import functools

import jax
import jax.numpy as jnp
from jax import lax
from jax.experimental import pallas as pl
from jax.experimental.pallas import tpu as pltpu
from jax.sharding import PartitionSpec as P

BF16 = jnp.bfloat16
F32 = jnp.float32
VERT = 32
TM = 16
YS = 8
XS = 4
CHUNKS = 4
WIDE = 256


def dot_last(left, right):
    return lax.dot_general(left, right, (((1,), (1,)), ((), ())), preferred_element_type=F32)


def dot_first(left, right):
    return lax.dot_general(left, right, (((0,), (0,)), ((), ())), preferred_element_type=F32)


def layer_kernel(
    feat, weight, heads, rows, edges, out,
    wg, hwg, proj, picked, recv, hid, xg, att, ret, sel, bias,
    w1_s, w1_r, wr_s, wr_r, wl_s, wl_r, wp_s, wp_r,
    hr_s, hr_r, hl_s, hl_r, x1_s, x1_r, x2_s, x2_r, hp_s, hp_r,
    b_s, b_r, g_s, g_r, a_s, a_r,
):
    v = lax.axis_index("vert")
    m = lax.axis_index("tm")
    y = m // 2
    c = m % 2
    x = v // 8
    z = v % 8

    def to_tm(yy, cc):
        return {"tm": lax.rem(yy + YS, YS) * 2 + cc}

    def copy(src, dst, ssem, rsem, dev):
        return pltpu.make_async_remote_copy(
            src_ref=src, dst_ref=dst, send_sem=ssem, recv_sem=rsem,
            device_id=dev, device_id_type=pl.DeviceIdType.MESH,
        )

    def loop(lo, hi, body):
        def step(i, carry):
            body(i)
            return carry
        lax.fori_loop(lo, hi, step, 0)

    barrier = pltpu.get_barrier_semaphore()
    loop(1, VERT, lambda k: pl.semaphore_signal(
        barrier, inc=1, device_id={"vert": lax.rem(v + k, VERT)}, device_id_type=pl.DeviceIdType.MESH))
    loop(1, TM, lambda k: pl.semaphore_signal(
        barrier, inc=1, device_id={"tm": lax.rem(m + k, TM)}, device_id_type=pl.DeviceIdType.MESH))
    pl.semaphore_wait(barrier, VERT + TM - 2)

    tile_cols = pl.ds(pl.multiple_of(y * 128, 128), 128)
    tile_rows = pl.ds(pl.multiple_of(c * 16, 16), 16)

    def w1(k, q):
        return copy(weight.at[tile_rows, tile_cols], wg.at[y, v, c], w1_s.at[k], w1_r.at[k], {"vert": q})

    def w1_in(k):
        q = lax.rem(v - k + VERT, VERT)
        return copy(weight.at[tile_rows, tile_cols], wg.at[y, q, c], w1_s.at[k], w1_r.at[k], {"vert": q})

    loop(1, VERT, lambda k: w1(k, lax.rem(v + k, VERT)).start())
    wg[y, v, c] = weight[tile_rows, tile_cols]
    hwg[y, c, x] = heads[x]
    sel[...] = (rows[...] == lax.broadcasted_iota(jnp.int32, (512, 512), 1)).astype(BF16)
    ri = lax.broadcasted_iota(jnp.int32, (256, 256), 0)
    ci = lax.broadcasted_iota(jnp.int32, (256, 256), 1)
    bias[...] = jnp.where(((ri & 15) == (ci & 15)) & (ri <= ci), 0.0, -1e30)
    loop(1, VERT, lambda k: w1_in(k).wait_recv())

    def pos(d):
        return lax.rem(y + d + 2 * YS, YS)

    def wpart(d, half):
        if half is None:
            return wg.at[pos(d), :, c]
        return wg.at[pos(d), pl.ds(half * 16, 16), c]

    def hpart(d, half):
        if half is None:
            return hwg.at[pos(d), c, x]
        return hwg.at[pos(d), c, x, :, pl.ds(half * 512, 512)]

    def up(part, s_sem, r_sem, s):
        half = 0 if s == 4 else None
        ref = part(1 - s, half)
        return copy(ref, ref, s_sem.at[s], r_sem.at[s], to_tm(y + 1, c))

    def up_in(part, s_sem, r_sem, s):
        half = 0 if s == 4 else None
        ref = part(-s, half)
        return copy(ref, ref, s_sem.at[s], r_sem.at[s], to_tm(y + 1, c))

    def down(part, s_sem, r_sem, s):
        half = 1 if s == 4 else None
        ref = part(s - 1, half)
        return copy(ref, ref, s_sem.at[s], r_sem.at[s], to_tm(y - 1, c))

    def down_in(part, s_sem, r_sem, s):
        half = 1 if s == 4 else None
        ref = part(s, half)
        return copy(ref, ref, s_sem.at[s], r_sem.at[s], to_tm(y - 1, c))

    def wpartner(d):
        ref = wg.at[pos(d), :, c]
        i = d % YS
        return copy(ref, ref, wp_s.at[i], wp_r.at[i], to_tm(y, 1 - c))

    def wpartner_in(d):
        ref = wg.at[pos(d), :, 1 - c]
        i = d % YS
        return copy(ref, ref, wp_s.at[i], wp_r.at[i], to_tm(y, 1 - c))

    for s in range(1, 5):
        up(wpart, wr_s, wr_r, s).start()
        down(wpart, wl_s, wl_r, s).start()
        if s == 1:
            wpartner(0).start()
        up_in(wpart, wr_s, wr_r, s).wait_recv()
        down_in(wpart, wl_s, wl_r, s).wait_recv()
        if s < 4:
            wpartner(-s).start()
            wpartner(s).start()
        else:
            wpartner(4).start()
    up(hpart, hr_s, hr_r, 1).start()
    down(hpart, hl_s, hl_r, 1).start()
    for d in range(YS):
        wpartner_in(d).wait_recv()

    def boundary(ch, k, q):
        return copy(picked.at[ch, q], recv.at[ch, v], b_s.at[ch, k], b_r.at[ch, k], {"vert": q})

    def boundary_in(ch, k):
        q = lax.rem(v - k + VERT, VERT)
        return copy(picked.at[ch, q], recv.at[ch, q], b_s.at[ch, k], b_r.at[ch, k], {"vert": q})

    for ch in range(CHUNKS):
        wide = jnp.concatenate(
            [wg[2 * ch].reshape(1024, 128), wg[2 * ch + 1].reshape(1024, 128)], axis=1)
        part = jnp.dot(feat[...], wide, preferred_element_type=F32).astype(BF16)
        proj[ch] = part
        rows_out = jnp.dot(sel[...], part, preferred_element_type=F32).astype(BF16)
        picked[ch] = rows_out.reshape(VERT, 16, WIDE)
        loop(1, VERT, lambda k: boundary(ch, k, lax.rem(v + k, VERT)).start())
        recv[ch, v] = picked[ch, v]

    for s in range(1, 5):
        up_in(hpart, hr_s, hr_r, s).wait_recv()
        down_in(hpart, hl_s, hl_r, s).wait_recv()
        if s < 4:
            up(hpart, hr_s, hr_r, s + 1).start()
            down(hpart, hl_s, hl_r, s + 1).start()

    xr = lax.rem(x + 1, XS)
    xl = lax.rem(x + 3, XS)
    xo = lax.rem(x + 2, XS)
    right = {"vert": xr * 8 + z}
    left = {"vert": xl * 8 + z}

    def x1(g, side):
        ref = hwg.at[pl.ds(2 * g, 2), c, x]
        return copy(ref, ref, x1_s.at[side, g], x1_r.at[side, g], right if side == 0 else left)

    def x1_in(g, side):
        ref = hwg.at[pl.ds(2 * g, 2), c, xl if side == 0 else xr]
        return copy(ref, ref, x1_s.at[side, g], x1_r.at[side, g], right if side == 0 else left)

    def x2(g, side):
        ref = hwg.at[2 * g + side, c, xl if side == 0 else xr]
        return copy(ref, ref, x2_s.at[side, g], x2_r.at[side, g], right if side == 0 else left)

    def x2_in(g, side):
        ref = hwg.at[2 * g + side, c, xo]
        return copy(ref, ref, x2_s.at[side, g], x2_r.at[side, g], right if side == 0 else left)

    def hpartner(g):
        ref = hwg.at[pl.ds(2 * g, 2), c]
        return copy(ref, ref, hp_s.at[g], hp_r.at[g], to_tm(y, 1 - c))

    def hpartner_in(g):
        ref = hwg.at[pl.ds(2 * g, 2), 1 - c]
        return copy(ref, ref, hp_s.at[g], hp_r.at[g], to_tm(y, 1 - c))

    for g in range(CHUNKS):
        x1(g, 0).start()
        x1(g, 1).start()

    def regroup(ch, k, t):
        return copy(hid.at[ch, t], xg.at[ch, :, m], g_s.at[ch, k], g_r.at[ch, k], {"tm": t})

    def regroup_in(ch, k):
        t = lax.rem(m - k + TM, TM)
        return copy(hid.at[ch, t], xg.at[ch, :, t], g_s.at[ch, k], g_r.at[ch, k], {"tm": t})

    for ch in range(CHUNKS):
        acc = proj[ch].astype(F32) + jnp.dot(edges[:, :512], proj[ch], preferred_element_type=F32)
        loop(1, VERT, lambda k: boundary_in(ch, k).wait_recv())
        acc = acc + jnp.dot(
            edges[:, 512:], recv[ch].reshape(512, WIDE), preferred_element_type=F32)
        hid[ch] = jnp.maximum(acc, 0.0).astype(BF16).reshape(TM, 2, 16, WIDE)
        loop(1, TM, lambda k: regroup(ch, k, lax.rem(m + k, TM)).start())
        xg[ch, :, m] = hid[ch, m]
        for side in range(2):
            x1_in(ch, side).wait_recv()
        for side in range(2):
            x2(ch, side).start()
    for side in range(2):
        x2_in(0, side).wait_recv()
    hpartner(0).start()
    for ch in range(CHUNKS):
        loop(1, TM, lambda k: regroup_in(ch, k).wait_recv())

    def give(g, k, t):
        return copy(att.at[g, :, t], ret.at[g, m], a_s.at[g, k], a_r.at[g, k], {"tm": t})

    def give_in(g, k):
        t = lax.rem(m - k + TM, TM)
        return copy(att.at[g, :, t], ret.at[g, t], a_s.at[g, k], a_r.at[g, k], {"tm": t})

    for g in range(CHUNKS):
        if g + 1 < CHUNKS:
            for side in range(2):
                x2_in(g + 1, side).wait_recv()
            hpartner(g + 1).start()
        hpartner_in(g).wait_recv()
        wide = hwg[pl.ds(2 * g, 2)].reshape(768, 1024)
        packed = dot_last(wide[:, :WIDE], xg[0].reshape(512, WIDE))
        for ch in range(1, CHUNKS):
            packed = packed + dot_last(
                wide[:, ch * WIDE:(ch + 1) * WIDE], xg[ch].reshape(512, WIDE))
        packed = packed.astype(BF16)
        for b in range(2):
            cols = slice(b * 256, (b + 1) * 256)
            outs = []
            for j in range(4):
                query = packed[192 * j:192 * j + 64, cols]
                key = packed[192 * j + 64:192 * j + 128, cols]
                value = packed[192 * j + 128:192 * j + 192, cols]
                score = dot_first(key, query) * 0.125 + bias[...]
                top = jnp.max(score, axis=0, keepdims=True)
                exponent = jnp.exp(score - top)
                scale = 1.0 / jnp.sum(exponent, axis=0, keepdims=True)
                attention = (exponent * scale).astype(BF16)
                outs.append(jnp.dot(value, attention, preferred_element_type=F32))
            block = jnp.concatenate(outs, axis=0)
            att[g, b] = block.T.astype(BF16).reshape(TM, 16, WIDE)
        loop(1, TM, lambda k: give(g, k, lax.rem(m + k, TM)).start())
        ret[g, m] = att[g, :, m]

    for g in range(CHUNKS):
        loop(1, TM, lambda k: give_in(g, k).wait_recv())
        total = hid[g].reshape(512, WIDE).astype(F32) + ret[g].reshape(512, WIDE).astype(F32)
        out[:, g * WIDE:(g + 1) * WIDE] = total.astype(BF16)

    loop(1, VERT, lambda k: w1_in(k).wait_send())
    for s in range(1, 5):
        up(wpart, wr_s, wr_r, s).wait_send()
        down(wpart, wl_s, wl_r, s).wait_send()
        up(hpart, hr_s, hr_r, s).wait_send()
        down(hpart, hl_s, hl_r, s).wait_send()
    for d in range(YS):
        wpartner(d).wait_send()
    for g in range(CHUNKS):
        for side in range(2):
            x1(g, side).wait_send()
            x2(g, side).wait_send()
        hpartner(g).wait_send()
        loop(1, VERT, lambda k: boundary_in(g, k).wait_send())
        loop(1, TM, lambda k: regroup_in(g, k).wait_send())
        loop(1, TM, lambda k: give_in(g, k).wait_send())


def layer(feat, weight, heads, rows, edges):
    dma = pltpu.SemaphoreType.DMA
    vmem = pl.BlockSpec(memory_space=pltpu.VMEM)
    return pl.pallas_call(
        layer_kernel,
        out_shape=jax.ShapeDtypeStruct((512, 1024), BF16),
        in_specs=[vmem] * 5,
        out_specs=vmem,
        scratch_shapes=[
            pltpu.VMEM((YS, VERT, 2, 16, 128), BF16),
            pltpu.VMEM((YS, 2, XS, 48, 1024), BF16),
            pltpu.VMEM((CHUNKS, 512, WIDE), BF16),
            pltpu.VMEM((CHUNKS, VERT, 16, WIDE), BF16),
            pltpu.VMEM((CHUNKS, VERT, 16, WIDE), BF16),
            pltpu.VMEM((CHUNKS, TM, 2, 16, WIDE), BF16),
            pltpu.VMEM((CHUNKS, 2, TM, 16, WIDE), BF16),
            pltpu.VMEM((CHUNKS, 2, TM, 16, WIDE), BF16),
            pltpu.VMEM((CHUNKS, TM, 2, 16, WIDE), BF16),
            pltpu.VMEM((512, 512), BF16),
            pltpu.VMEM((256, 256), F32),
            dma((VERT,)), dma((VERT,)),
            dma((5,)), dma((5,)), dma((5,)), dma((5,)), dma((YS,)), dma((YS,)),
            dma((5,)), dma((5,)), dma((5,)), dma((5,)),
            dma((2, CHUNKS)), dma((2, CHUNKS)), dma((2, CHUNKS)), dma((2, CHUNKS)),
            dma((CHUNKS,)), dma((CHUNKS,)),
            dma((CHUNKS, VERT)), dma((CHUNKS, VERT)),
            dma((CHUNKS, TM)), dma((CHUNKS, TM)),
            dma((CHUNKS, TM)), dma((CHUNKS, TM)),
        ],
        compiler_params=pltpu.CompilerParams(
            collective_id=0, has_side_effects=True, vmem_limit_bytes=56 * 1024 * 1024),
    )(feat, weight, heads, rows, edges)


def shards(features, graph_weight, head_weight, send_rows, send_count, block_index, block_values):
    live = jnp.arange(16)[None, :] < send_count[0, 0][:, None]
    rows = jnp.where(live, send_rows[0, 0], -1).reshape(512, 1)
    edge = block_values[0].reshape(4, 128, 3, 128)
    place = block_index[0][:, None, :, None] == jnp.arange(8)[None, None, None, :]
    zero = jnp.zeros((), BF16)
    edges = sum(
        jnp.where(place[:, :, k, :, None], edge[:, :, k, None, :], zero) for k in range(3)
    ).reshape(512, 1024)
    heads = head_weight[0].reshape(XS, 48, 1024)
    return layer(features[0], graph_weight, heads, rows, edges)[None]


def solution(mesh):
    return jax.shard_map(
        shards,
        mesh=mesh,
        in_specs=(
            P("tm", "vert", None),
            P("vert", None),
            P("tm", None, None),
            P("tm", "vert", None, None),
            P("tm", "vert", None),
            P("tm", "vert", None),
            P("tm", "vert", None, None),
        ),
        out_specs=P("tm", "vert", None),
        check_vma=False,
    )
```

time: 264 us -> 136 us (0.52)
  waiting for transfers between devices: 133 us -> 0 us
  Pallas kernels: 0 us -> 129 us
  blocking collectives: 31.7 us -> 0 us
  starting transfers between devices: 22.7 us -> 0 us
  matrix products: 21 us -> 0 us
  local copies, waits for them, and re-layouts: 24.9 us -> 5.41 us
  other arithmetic: 16.2 us -> 1.36 us
  between operations: 13.5 us -> 0.05 us
    pallas_call x0 -> x1, Pallas kernels: none -> 129 us  [layer(): pl.pallas_call(layer_kernel, out_shape=jax.ShapeDtypeStruct((512, 1024),...]
    all_gather x2 -> x0, waiting for transfers between devices: 84.7 us -> none  [the longest x1 84.7 us: shards(): lax.all_gather(graph_weight, 'vert', axis=0, tiled=True)]
    all_to_all x2 -> x0, waiting for transfers between devices: 47 us -> none  [the longest x1 28 us: shards(): lax.all_to_all(hidden[None], 'tm', split_axis=1, concat_axis=0, tiled=True)]
    all_to_all x1 -> x0, blocking collectives: 31.7 us -> none  [shards(): lax.all_to_all(attended, 'tm', split_axis=0, concat_axis=1, tiled=True)]
    all_to_all x2 -> x0, starting transfers between devices: 22.7 us -> none  [the longest x1 16.7 us: shards(): lax.all_to_all(hidden[None], 'tm', split_axis=1, concat_axis=0, tiled=True)]
    dot_general x5 -> x0, matrix products: 21 us -> none  [the longest x1 7.53 us: attend_heads(): jnp.einsum('tvd,hcd->tvhc', regrouped, head_piece, preferred_element_type...]
    unnamed x1 -> x0, other arithmetic: 8.09 us -> none
    gather x2 -> x0, local copies, waits for them, and re-layouts: 6.29 us -> none  [the longest x1 4.24 us: shards(): jnp.take(columns, index_list.reshape(-1), axis=0)]
  transfers between devices with their start and end apart: 4 -> 0, of which waited for: 3 -> 0; matrix products, arithmetic and copies ran while one was open for 14% -> 0% of each run, Pallas kernels for 0% -> 0%
where the time goes in v1:
time: 136 us
  Pallas kernels  129 us (95%)
  local copies, waits for them, and re-layouts  5.41 us (4%)
  other arithmetic  1.36 us (1%)
    pallas_call x1, Pallas kernels, layer(): pl.pallas_call(layer_kernel, out_shape=jax.ShapeDtypeStruct((512, 1024),...  129 us
    unnamed x11, local copies, waits for them, and re-layouts  5.03 us

profile of v1, /device:TPU:1, one launch (start us, length us, event | category | flops | bytes accessed | tf_op | source)
XLA Modules:
  0.0 136.2 jit_solution(2897430444056458034)
XLA Ops:
  0.0 0.0 copy-start.2
  0.0 0.7 copy-done.2
  0.7 0.0 copy-start.1
  0.7 0.1 iota_compare_fusion.1
  0.8 0.0 copy-start.3
  0.8 0.7 copy-done.3
  1.4 0.1 iota_compare_fusion
  1.5 0.0 copy-done.1
  1.5 0.1 copy.11
  1.6 0.2 lt.30
  1.8 0.0 copy-start
  1.8 0.2 squeeze.8
  1.9 0.7 broadcast_select_fusion.rows
  2.7 0.1 copy-done
  2.8 0.5 select_add_fusion
  3.3 1.2 copy.20
  4.5 129.4 %shard_map.73 = bf16[512,1024]{1,0:T(8,128)(2,1)} custom-call(bf16[512,1024]{1,0:T(8,128)(2,1)} %bitcast.31, bf16[32,1024]{1,0:T(8,128)(2,1)} %weight.1, bf16[4,48,1024]{2,1,0:T(8,128)(2,1)} %bitcast.32, s32[512,1]{1,0:T(8,128)} %broadcast_select_fusion.rows, bf16[512,1024]{1,0:T(8,128)(2,1)} %bitcast.29), custom_call_target="tpu_custom_call" | custom-call | tf_op jit(solution)/shard_map/pallas_call | solution.py:289
  133.9 2.3 %copy.23 = bf16[1,512,1024]{2,1,0:T(8,128)(2,1)} copy(bf16[1,512,1024]{2,1,0:T(8,128)(2,1)} %bitcast.30) | data formatting | bytes 2097152
  (3 shorter events, 0.0 us)
Async XLA Ops:
  0.0 0.7 copy-start.2
  0.7 0.8 copy-start.1
  0.8 0.7 copy-start.3
  1.8 1.0 copy-start

commit v2 on v0

v2 whole, which is shorter than its diff:
```python
import jax
import jax.numpy as jnp
from jax import lax
from jax.experimental import pallas as pl
from jax.experimental.pallas import tpu as pltpu
from jax.sharding import PartitionSpec as P

BF16 = jnp.bfloat16
F32 = jnp.float32
VERT = 32
TM = 16
YS = 8
XS = 4
WIDE = 256
STEPS = 5
MESH = pl.DeviceIdType.MESH


def dot_last(left, right):
    return lax.dot_general(left, right, (((1,), (1,)), ((), ())), preferred_element_type=F32)


def dot_first(left, right):
    return lax.dot_general(left, right, (((0,), (0,)), ((), ())), preferred_element_type=F32)


def far_first(i, size):
    return lax.rem(size // 2 + (1 - 2 * lax.rem(i, 2)) * ((i + 1) // 2) + size, size)


def layer_kernel(
    feat_in, weight_in, heads, rows_in, count_in, blocks_in, index_in, out,
    feat, weight, rows, count, blocks, index,
    wg, hwg, proj_one, proj_two, picked_one, picked_two, recv_one, recv_two,
    hid, xg, att, ret, sel, edges, bias,
    in_s, w1_s, w1_r, wr_s, wr_r, wl_s, wl_r, wp_s, wp_r,
    hr_s, hr_r, hl_s, hl_r, x1_s, x1_r, x2_s, x2_r, hp_s, hp_r,
    b_s, b_r, g_s, g_r, a_s, a_r,
):
    v = lax.axis_index("vert")
    m = lax.axis_index("tm")
    y = m // 2
    c = lax.rem(m, 2)
    x = v // 8
    z = lax.rem(v, 8)

    def pos(d):
        return lax.rem(y + d + 2 * YS, YS)

    def to_tm(d, cc):
        return {"tm": pos(d) * 2 + cc}

    def copy(src, dst, ssem, rsem, dev):
        return pltpu.make_async_remote_copy(
            src_ref=src, dst_ref=dst, send_sem=ssem, recv_sem=rsem,
            device_id=dev, device_id_type=MESH,
        )

    def loop(lo, hi, body):
        def step(i, carry):
            body(i)
            return carry
        lax.fori_loop(lo, hi, step, 0)

    def vert_peers(body):
        def one(i):
            dx, dz = far_first(i // 8, XS), far_first(lax.rem(i, 8), 8)
            body(lax.rem(x + dx, XS) * 8 + lax.rem(z + dz, 8))
        loop(0, VERT - 1, one)

    def tm_peers(body):
        def one(i):
            body(pos(far_first(i // 2, YS)) * 2 + lax.rem(c + 1 + lax.rem(i, 2), 2))
        loop(0, TM - 1, one)

    barrier = pltpu.get_barrier_semaphore()
    vert_peers(lambda q: pl.semaphore_signal(barrier, inc=1, device_id={"vert": q}, device_id_type=MESH))
    tm_peers(lambda t: pl.semaphore_signal(barrier, inc=1, device_id={"tm": t}, device_id_type=MESH))

    loads = [
        pltpu.make_async_copy(src, dst, in_s.at[i]) for i, (src, dst) in enumerate((
            (rows_in, rows), (count_in, count), (index_in, index), (blocks_in, blocks),
            (weight_in, weight), (heads.at[x], hwg.at[y, c, x]), (feat_in, feat)))
    ]
    for load in loads:
        load.start()

    tile_cols = pl.ds(pl.multiple_of(y * 128, 128), 128)
    tile_rows = pl.ds(pl.multiple_of(c * 16, 16), 16)

    with jax.named_scope("tables"):
        ri = lax.broadcasted_iota(jnp.int32, (256, 256), 0)
        ci = lax.broadcasted_iota(jnp.int32, (256, 256), 1)
        bias[...] = jnp.where(((ri & 15) == (ci & 15)) & (ri <= ci), 0.0, -1e30)
        for load in loads[:5]:
            load.wait()
        wg[y, v, c] = weight[tile_rows, tile_cols]
        live = lax.broadcasted_iota(jnp.int32, (16, VERT), 0) < count[...]
        slots = jnp.where(live, rows[...], 1023)
        lane = lax.broadcasted_iota(jnp.int32, (VERT, 512), 1)
        spread = (lane // 16 == lax.broadcasted_iota(jnp.int32, (VERT, 512), 0)).astype(BF16)
        high = jnp.dot((slots >> 4).astype(F32).astype(BF16), spread, preferred_element_type=F32)
        low = jnp.dot((slots & 15).astype(F32).astype(BF16), spread, preferred_element_type=F32)
        slot = lax.broadcasted_iota(jnp.int32, (16, 512), 0)
        mine = slot == (lax.broadcasted_iota(jnp.int32, (16, 512), 1) & 15)
        wanted = jnp.sum(jnp.where(mine, high * 16.0 + low, 0.0), axis=0, keepdims=True)
        vertex = lax.broadcasted_iota(jnp.int32, (512, 512), 0).astype(F32)
        sel[...] = jnp.where(vertex == wanted, 1.0, 0.0).T.astype(BF16)
        for r in range(4):
            band = slice(r * 128, (r + 1) * 128)
            pieces = [blocks[k, band] for k in range(3)]
            zero = jnp.zeros((128, 128), BF16)
            for b in range(8):
                block = zero
                for k in range(3):
                    block = jnp.where(index[k, 0, r] == b, pieces[k], block)
                edges[band, b * 128:(b + 1) * 128] = block
        loads[5].wait()
    with jax.named_scope("entry"):
        pl.semaphore_wait(barrier, VERT + TM - 2)

    def w1(q):
        return copy(weight.at[tile_rows, tile_cols], wg.at[y, v, c], w1_s.at[0], w1_r.at[0], {"vert": q})

    def w1_all():
        ref = wg.at[y, pl.ds(0, VERT - 1), c]
        return copy(ref, ref, w1_s.at[0], w1_r.at[0], {"vert": lax.rem(v + 1, VERT)})

    def wpart(d, half):
        if half is None:
            return wg.at[pos(d), :, c]
        return wg.at[pos(d), pl.ds(half * 16, 16), c]

    def hpart(d, half):
        if half is None:
            return hwg.at[pos(d), c, x]
        return hwg.at[pos(d), c, x, :, pl.ds(half * 512, 512)]

    def up(part, sems, s):
        ref = part(1 - s, 0 if s == 4 else None)
        return copy(ref, ref, sems[0].at[s], sems[1].at[s], to_tm(1, c))

    def up_in(part, sems, s):
        ref = part(-s, 0 if s == 4 else None)
        return copy(ref, ref, sems[0].at[s], sems[1].at[s], to_tm(1, c))

    def down(part, sems, s):
        ref = part(s - 1, 1 if s == 4 else None)
        return copy(ref, ref, sems[0].at[s], sems[1].at[s], to_tm(-1, c))

    def down_in(part, sems, s):
        ref = part(s, 1 if s == 4 else None)
        return copy(ref, ref, sems[0].at[s], sems[1].at[s], to_tm(-1, c))

    wup, wdown = (wr_s, wr_r), (wl_s, wl_r)
    hup, hdown = (hr_s, hr_r), (hl_s, hl_r)

    def ring_send(part, sems_up, sems_down, s):
        up(part, sems_up, s).start()
        down(part, sems_down, s).start()

    def ring_wait(part, sems_up, sems_down, s):
        up_in(part, sems_up, s).wait_recv()
        down_in(part, sems_down, s).wait_recv()

    def wpartner(d):
        ref = wg.at[pos(d), :, c]
        i = d % YS
        return copy(ref, ref, wp_s.at[i], wp_r.at[i], to_tm(0, 1 - c))

    def wpartner_in(d):
        ref = wg.at[pos(d), :, 1 - c]
        i = d % YS
        return copy(ref, ref, wp_s.at[i], wp_r.at[i], to_tm(0, 1 - c))

    def tiles(s):
        return (0,) if s == 0 else (4,) if s == 4 else (-s, s)

    def store(s, one, two):
        if s == 0:
            return one.at[0]
        if s == 4:
            return one.at[1]
        return two.at[s - 1]

    def width(s):
        return 128 * len(tiles(s))

    def boundary(s, q):
        return copy(store(s, picked_one, picked_two).at[q], store(s, recv_one, recv_two).at[v],
                    b_s.at[s], b_r.at[s], {"vert": q})

    def boundary_all(s):
        most = pl.ds(0, VERT - 1)
        return copy(store(s, picked_one, picked_two).at[most], store(s, recv_one, recv_two).at[most],
                    b_s.at[s], b_r.at[s], {"vert": lax.rem(v + 1, VERT)})

    def project(s):
        with jax.named_scope(f"project{s}"):
            parts = [wg[pos(d)].reshape(1024, 128) for d in tiles(s)]
            wide = parts[0] if len(parts) == 1 else jnp.concatenate(parts, axis=1)
            part = jnp.dot(feat[...], wide, preferred_element_type=F32).astype(BF16)
            store(s, proj_one, proj_two)[...] = part
            rows_out = jnp.dot(sel[...], part, preferred_element_type=F32).astype(BF16)
            picked = store(s, picked_one, picked_two)
            picked[...] = rows_out.reshape(VERT, 16, width(s))
            vert_peers(lambda q: boundary(s, q).start())
            store(s, recv_one, recv_two)[v] = picked[v]

    def regroup(ct, t):
        return copy(hid.at[ct, t], xg.at[ct, :, m], g_s.at[0], g_r.at[0], {"tm": t})

    def regroup_all():
        return copy(hid.at[:, pl.ds(0, TM - 1)], hid.at[:, pl.ds(0, TM - 1)],
                    g_s.at[0], g_r.at[0], to_tm(1, c))

    def convolve(s):
        with jax.named_scope(f"bwait{s}"):
            boundary_all(s).wait_recv()
        with jax.named_scope(f"convolve{s}"):
            part = store(s, proj_one, proj_two)[...]
            acc = part.astype(F32) + jnp.dot(edges[:, :512], part, preferred_element_type=F32)
            acc = acc + jnp.dot(
                edges[:, 512:], store(s, recv_one, recv_two)[...].reshape(512, width(s)),
                preferred_element_type=F32)
            done = jnp.maximum(acc, 0.0).astype(BF16)
            for i, d in enumerate(tiles(s)):
                hid[pos(d)] = done[:, i * 128:(i + 1) * 128].reshape(TM, 2, 16, 128)
            for d in tiles(s):
                tm_peers(lambda t: regroup(pos(d), t).start())
                xg[pos(d), :, m] = hid[pos(d), m]

    xr = lax.rem(x + 1, XS)
    xl = lax.rem(x + 3, XS)
    xo = lax.rem(x + 2, XS)
    sides = ({"vert": xr * 8 + z}, {"vert": xl * 8 + z})

    def x1(d, side):
        ref = hwg.at[pos(d), c, x]
        return copy(ref, ref, x1_s.at[side, d % YS], x1_r.at[side, d % YS], sides[side])

    def x1_in(d, side):
        ref = hwg.at[pos(d), c, (xl, xr)[side]]
        return copy(ref, ref, x1_s.at[side, d % YS], x1_r.at[side, d % YS], sides[side])

    def x2(d, side):
        ref = hwg.at[pos(d), c, (xl, xr)[side], :, pl.ds(512 * side, 512)]
        return copy(ref, ref, x2_s.at[side, d % YS], x2_r.at[side, d % YS], sides[side])

    def x2_in(d, side):
        ref = hwg.at[pos(d), c, xo, :, pl.ds(512 * side, 512)]
        return copy(ref, ref, x2_s.at[side, d % YS], x2_r.at[side, d % YS], sides[side])

    def hpartner(d):
        ref = hwg.at[pos(d), c]
        return copy(ref, ref, hp_s.at[d % YS], hp_r.at[d % YS], to_tm(0, 1 - c))

    def hpartner_in(d):
        ref = hwg.at[pos(d), 1 - c]
        return copy(ref, ref, hp_s.at[d % YS], hp_r.at[d % YS], to_tm(0, 1 - c))

    def x1_send(s):
        for d in tiles(s):
            for side in range(2):
                x1(d, side).start()

    def x2_send(s):
        with jax.named_scope(f"xwait{s}"):
            for d in tiles(s):
                for side in range(2):
                    x1_in(d, side).wait_recv()
                for side in range(2):
                    x2(d, side).start()

    def xdone(s):
        with jax.named_scope(f"xdone{s}"):
            for d in tiles(s):
                for side in range(2):
                    x2_in(d, side).wait_recv()
                hpartner(d).start()

    def wstep(s):
        with jax.named_scope(f"wstep{s}"):
            ring_wait(wpart, wup, wdown, s)
            if s < 4:
                ring_send(wpart, wup, wdown, s + 1)
            for d in tiles(s):
                wpartner(d).start()

    def hstep(s):
        with jax.named_scope(f"hstep{s}"):
            ring_wait(hpart, hup, hdown, s)
            if s < 4:
                ring_send(hpart, hup, hdown, s + 1)
        x1_send(s)

    def wready(s):
        with jax.named_scope(f"wready{s}"):
            for d in tiles(s):
                wpartner_in(d).wait_recv()

    vert_peers(lambda q: w1(q).start())
    ring_send(hpart, hup, hdown, 1)
    x1_send(0)
    hstep(1)
    with jax.named_scope("wtiles"):
        w1_all().wait_recv()
    ring_send(wpart, wup, wdown, 1)
    wpartner(0).start()
    loads[6].wait()
    wready(0)
    project(0)
    hstep(2)
    x2_send(0)
    x2_send(1)
    wstep(1)
    wready(1)
    project(1)
    hstep(3)
    convolve(0)
    wstep(2)
    x2_send(2)
    wready(2)
    project(2)
    hstep(4)
    wstep(3)
    wready(3)
    project(3)
    x2_send(3)
    convolve(1)
    xdone(0)
    xdone(1)
    wstep(4)
    wready(4)
    project(4)
    x2_send(4)
    convolve(2)
    xdone(2)
    convolve(3)
    xdone(3)
    convolve(4)
    xdone(4)
    with jax.named_scope("hready"):
        for d in range(YS):
            hpartner_in(d).wait_recv()
    with jax.named_scope("gwait"):
        regroup_all().wait_recv()

    def give(g, t):
        return copy(att.at[g, :, t], ret.at[g, m], a_s.at[0], a_r.at[g], {"tm": t})

    def give_all(g):
        most = pl.ds(0, TM - 1)
        return copy(ret.at[g, most], ret.at[g, most], a_s.at[0], a_r.at[g], to_tm(1, c))

    def give_out():
        most = pl.ds(0, TM - 1)
        return copy(ret.at[:, most], ret.at[:, most], a_s.at[0], a_r.at[0], to_tm(1, c))

    def attend(g):
        with jax.named_scope("attend"):
            wide = hwg[g].reshape(384, 1024)
            packed = None
            for ch in range(4):
                seen = jnp.concatenate(
                    [xg[2 * ch].reshape(512, 128), xg[2 * ch + 1].reshape(512, 128)], axis=1)
                term = dot_last(wide[:, ch * WIDE:(ch + 1) * WIDE], seen)
                packed = term if packed is None else packed + term
            packed = packed.astype(BF16)
            for b in range(2):
                cols = slice(b * 256, (b + 1) * 256)
                outs = []
                for j in range(2):
                    query = packed[192 * j:192 * j + 64, cols]
                    key = packed[192 * j + 64:192 * j + 128, cols]
                    value = packed[192 * j + 128:192 * j + 192, cols]
                    score = dot_first(key, query) * 0.125 + bias[...]
                    top = jnp.max(score, axis=0, keepdims=True)
                    exponent = jnp.exp(score - top)
                    scale = 1.0 / jnp.sum(exponent, axis=0, keepdims=True)
                    attention = (exponent * scale).astype(BF16)
                    outs.append(jnp.dot(value, attention, preferred_element_type=F32))
                block = jnp.concatenate(outs, axis=0)
                att[g, b] = block.T.astype(BF16).reshape(TM, 16, 128)
            tm_peers(lambda t: give(g, t).start())
            ret[g, m] = att[g, :, m]

    loop(0, YS, attend)

    with jax.named_scope("sent"):
        w1_all().wait_send()
        for s in range(1, 5):
            up(wpart, wup, s).wait_send()
            down(wpart, wdown, s).wait_send()
            up(hpart, hup, s).wait_send()
            down(hpart, hdown, s).wait_send()
        for d in range(YS):
            wpartner(d).wait_send()
            for side in range(2):
                x1(d, side).wait_send()
                x2(d, side).wait_send()
            hpartner(d).wait_send()
        for s in range(STEPS):
            boundary_all(s).wait_send()
        regroup_all().wait_send()

    def finish(g):
        with jax.named_scope("await"):
            give_all(g).wait_recv()
        total = hid[g].reshape(512, 128).astype(F32) + ret[g].reshape(512, 128).astype(F32)
        out[:, pl.ds(pl.multiple_of(g * 128, 128), 128)] = total.astype(BF16)

    loop(0, YS, finish)
    with jax.named_scope("last"):
        give_out().wait_send()


def layer(*operands):
    dma = pltpu.SemaphoreType.DMA
    vmem = pl.BlockSpec(memory_space=pltpu.VMEM)
    hbm = pl.BlockSpec(memory_space=pltpu.HBM)
    return pl.pallas_call(
        layer_kernel,
        out_shape=jax.ShapeDtypeStruct((512, 1024), BF16),
        in_specs=[hbm] * 7,
        out_specs=vmem,
        scratch_shapes=[
            pltpu.VMEM((512, 1024), BF16),
            pltpu.VMEM((32, 1024), BF16),
            pltpu.VMEM((16, VERT), jnp.int32),
            pltpu.VMEM((1, VERT), jnp.int32),
            pltpu.VMEM((3, 512, 128), BF16),
            pltpu.SMEM((3, 1, 4), jnp.int32),
            pltpu.VMEM((YS, VERT, 2, 16, 128), BF16),
            pltpu.VMEM((YS, 2, XS, 48, 1024), BF16),
            pltpu.VMEM((2, 512, 128), BF16),
            pltpu.VMEM((3, 512, WIDE), BF16),
            pltpu.VMEM((2, VERT, 16, 128), BF16),
            pltpu.VMEM((3, VERT, 16, WIDE), BF16),
            pltpu.VMEM((2, VERT, 16, 128), BF16),
            pltpu.VMEM((3, VERT, 16, WIDE), BF16),
            pltpu.VMEM((YS, TM, 2, 16, 128), BF16),
            pltpu.VMEM((YS, 2, TM, 16, 128), BF16),
            pltpu.VMEM((YS, 2, TM, 16, 128), BF16),
            pltpu.VMEM((YS, TM, 2, 16, 128), BF16),
            pltpu.VMEM((512, 512), BF16),
            pltpu.VMEM((512, 1024), BF16),
            pltpu.VMEM((256, 256), F32),
            dma((7,)), dma((1,)), dma((1,)),
            dma((5,)), dma((5,)), dma((5,)), dma((5,)), dma((YS,)), dma((YS,)),
            dma((5,)), dma((5,)), dma((5,)), dma((5,)),
            dma((2, YS)), dma((2, YS)), dma((2, YS)), dma((2, YS)),
            dma((YS,)), dma((YS,)),
            dma((STEPS,)), dma((STEPS,)),
            dma((1,)), dma((1,)),
            dma((1,)), dma((YS,)),
        ],
        compiler_params=pltpu.CompilerParams(
            collective_id=0, has_side_effects=True, vmem_limit_bytes=48 * 1024 * 1024),
    )(*(pltpu.with_memory_space_constraint(op, pltpu.HBM) for op in operands))


def shards(features, graph_weight, head_weight, send_rows, send_count, block_index, block_values):
    heads = head_weight[0].reshape(XS, 48, 1024)
    return layer(
        features[0], graph_weight, heads, send_rows[0, 0].T, send_count[0],
        block_values[0].transpose(1, 0, 2), block_index.transpose(2, 0, 1))[None]


def solution(mesh):
    return jax.shard_map(
        shards,
        mesh=mesh,
        in_specs=(
            P("tm", "vert", None),
            P("vert", None),
            P("tm", None, None),
            P("tm", "vert", None, None),
            P("tm", "vert", None),
            P("tm", "vert", None),
            P("tm", "vert", None, None),
        ),
        out_specs=P("tm", "vert", None),
        check_vma=False,
    )
```

time: 264 us -> 101 us (0.38)
  waiting for transfers between devices: 133 us -> 0 us
  Pallas kernels: 0 us -> 99.7 us
  blocking collectives: 31.7 us -> 0 us
  local copies, waits for them, and re-layouts: 24.9 us -> 0.97 us
  starting transfers between devices: 22.7 us -> 0 us
  matrix products: 21 us -> 0 us
  other arithmetic: 16.2 us -> 0 us
  between operations: 13.5 us -> 0.01 us
    pallas_call x0 -> x1, Pallas kernels: none -> 99.7 us  [layer(): pl.pallas_call(layer_kernel, out_shape=jax.ShapeDtypeStruct((512, 1024),...]
    all_gather x2 -> x0, waiting for transfers between devices: 84.7 us -> none  [the longest x1 84.7 us: shards(): lax.all_gather(graph_weight, 'vert', axis=0, tiled=True)]
    all_to_all x2 -> x0, waiting for transfers between devices: 47 us -> none  [the longest x1 28 us: shards(): lax.all_to_all(hidden[None], 'tm', split_axis=1, concat_axis=0, tiled=True)]
    all_to_all x1 -> x0, blocking collectives: 31.7 us -> none  [shards(): lax.all_to_all(attended, 'tm', split_axis=0, concat_axis=1, tiled=True)]
    all_to_all x2 -> x0, starting transfers between devices: 22.7 us -> none  [the longest x1 16.7 us: shards(): lax.all_to_all(hidden[None], 'tm', split_axis=1, concat_axis=0, tiled=True)]
    dot_general x5 -> x0, matrix products: 21 us -> none  [the longest x1 7.53 us: attend_heads(): jnp.einsum('tvd,hcd->tvhc', regrouped, head_piece, preferred_element_type...]
    unnamed x1 -> x0, other arithmetic: 8.09 us -> none
    unnamed x12 -> x1, local copies, waits for them, and re-layouts: 8.44 us -> 0.97 us
  transfers between devices with their start and end apart: 4 -> 0, of which waited for: 3 -> 0; matrix products, arithmetic and copies ran while one was open for 14% -> 0% of each run, Pallas kernels for 0% -> 0%
where the time goes in v2:
time: 101 us
  Pallas kernels  99.7 us (99%)
    pallas_call x1, Pallas kernels, layer(): pl.pallas_call(layer_kernel, out_shape=jax.ShapeDtypeStruct((512, 1024),...  99.7 us

profile of v2, /device:TPU:1, one launch (start us, length us, event | category | flops | bytes accessed | tf_op | source)
XLA Modules:
  0.0 100.6 jit_solution(15362339596022214814)
XLA Ops:
  0.0 99.7 %shard_map.73 = bf16[512,1024]{1,0:T(8,128)(2,1)S(1)} custom-call(bf16[512,1024]{1,0:T(8,128)(2,1)} %bitcast.12, bf16[32,1024]{1,0:T(8,128)(2,1)} %weight_in.1, bf16[4,48,1024]{2,1,0:T(8,128)(2,1)} %bitcast.13, s32[16,32]{1,0:T(8,128)} %bitcast.15, s32[1,32]{1,0:T(1,128)} %bitcast.17, bf16[3,512,128]{2,1,0:T(8,128)(2,1)} %bitcast.14, s32[3,1,4]{2,1,0:T(1,128)} %bitcast.16), custom_call_target="tpu_custom_call" | custom-call | tf_op jit(solution)/shard_map/pallas_call | solution.py:422
  99.7 1.0 copy.9

commit v3 on v2

--- a/solution.py
+++ b/solution.py
@@ -24,16 +24,12 @@
     return lax.dot_general(left, right, (((0,), (0,)), ((), ())), preferred_element_type=F32)
 
 
-def far_first(i, size):
-    return lax.rem(size // 2 + (1 - 2 * lax.rem(i, 2)) * ((i + 1) // 2) + size, size)
-
-
 def layer_kernel(
     feat_in, weight_in, heads, rows_in, count_in, blocks_in, index_in, out,
     feat, weight, rows, count, blocks, index,
     wg, hwg, proj_one, proj_two, picked_one, picked_two, recv_one, recv_two,
     hid, xg, att, ret, sel, edges, bias,
-    in_s, w1_s, w1_r, wr_s, wr_r, wl_s, wl_r, wp_s, wp_r,
+    in_s, w1_s, w1_r, wr_s, wr_r, wp_s, wp_r,
     hr_s, hr_r, hl_s, hl_r, x1_s, x1_r, x2_s, x2_r, hp_s, hp_r,
     b_s, b_r, g_s, g_r, a_s, a_r,
 ):
@@ -62,16 +58,19 @@
             return carry
         lax.fori_loop(lo, hi, step, 0)
 
+    by_x = [lax.rem(x + dx, XS) * 8 for dx in range(XS)]
+    by_z = [lax.rem(z + dz, 8) for dz in range(8)]
+    vert_ids = [by_x[dx] + by_z[dz] for dx in (2, 1, 3, 0) for dz in (4, 3, 5, 2, 6, 1, 7, 0)][:-1]
+    by_y = [lax.rem(y + dy, YS) * 2 for dy in range(YS)]
+    tm_ids = [by_y[dy] + cc for dy in (4, 3, 5, 2, 6, 1, 7, 0) for cc in (1 - c, c)][:-1]
+
     def vert_peers(body):
-        def one(i):
-            dx, dz = far_first(i // 8, XS), far_first(lax.rem(i, 8), 8)
-            body(lax.rem(x + dx, XS) * 8 + lax.rem(z + dz, 8))
-        loop(0, VERT - 1, one)
+        for q in vert_ids:
+            body(q)
 
     def tm_peers(body):
-        def one(i):
-            body(pos(far_first(i // 2, YS)) * 2 + lax.rem(c + 1 + lax.rem(i, 2), 2))
-        loop(0, TM - 1, one)
+        for t in tm_ids:
+            body(t)
 
     barrier = pltpu.get_barrier_semaphore()
     vert_peers(lambda q: pl.semaphore_signal(barrier, inc=1, device_id={"vert": q}, device_id_type=MESH))
@@ -85,7 +84,7 @@
     for load in loads:
         load.start()
 
-    tile_cols = pl.ds(pl.multiple_of(y * 128, 128), 128)
+    tile_cols = [pl.ds(pl.multiple_of(pos(4 * i) * 128, 128), 128) for i in range(2)]
     tile_rows = pl.ds(pl.multiple_of(c * 16, 16), 16)
 
     with jax.named_scope("tables"):
@@ -94,7 +93,8 @@
         bias[...] = jnp.where(((ri & 15) == (ci & 15)) & (ri <= ci), 0.0, -1e30)
         for load in loads[:5]:
             load.wait()
-        wg[y, v, c] = weight[tile_rows, tile_cols]
+        for i in range(2):
+            wg[pos(4 * i), v, c] = weight[tile_rows, tile_cols[i]]
         live = lax.broadcasted_iota(jnp.int32, (16, VERT), 0) < count[...]
         slots = jnp.where(live, rows[...], 1023)
         lane = lax.broadcasted_iota(jnp.int32, (VERT, 512), 1)
@@ -119,17 +119,21 @@
     with jax.named_scope("entry"):
         pl.semaphore_wait(barrier, VERT + TM - 2)
 
-    def w1(q):
-        return copy(weight.at[tile_rows, tile_cols], wg.at[y, v, c], w1_s.at[0], w1_r.at[0], {"vert": q})
-
-    def w1_all():
-        ref = wg.at[y, pl.ds(0, VERT - 1), c]
-        return copy(ref, ref, w1_s.at[0], w1_r.at[0], {"vert": lax.rem(v + 1, VERT)})
-
-    def wpart(d, half):
-        if half is None:
-            return wg.at[pos(d), :, c]
-        return wg.at[pos(d), pl.ds(half * 16, 16), c]
+    def w1(i, q):
+        return copy(weight.at[tile_rows, tile_cols[i]], wg.at[pos(4 * i), v, c],
+                    w1_s.at[i], w1_r.at[i], {"vert": q})
+
+    def w1_all(i):
+        ref = wg.at[pos(4 * i), pl.ds(0, VERT - 1), c]
+        return copy(ref, ref, w1_s.at[i], w1_r.at[i], {"vert": lax.rem(v + 1, VERT)})
+
+    def wring(s, h, side):
+        ref = wg.at[pos((1 - s, s - 1)[side]), pl.ds(16 * h, 16), c]
+        return copy(ref, ref, wr_s.at[side, s, h], wr_r.at[side, s, h], to_tm(1 - 2 * side, c))
+
+    def wring_in(s, h, side):
+        ref = wg.at[pos((-s, s)[side]), pl.ds(16 * h, 16), c]
+        return copy(ref, ref, wr_s.at[side, s, h], wr_r.at[side, s, h], to_tm(1 - 2 * side, c))
 
     def hpart(d, half):
         if half is None:
@@ -152,7 +156,6 @@
         ref = part(s, 1 if s == 4 else None)
         return copy(ref, ref, sems[0].at[s], sems[1].at[s], to_tm(-1, c))
 
-    wup, wdown = (wr_s, wr_r), (wl_s, wl_r)
     hup, hdown = (hr_s, hr_r), (hl_s, hl_r)
 
     def ring_send(part, sems_up, sems_down, s):
@@ -281,9 +284,12 @@
 
     def wstep(s):
         with jax.named_scope(f"wstep{s}"):
-            ring_wait(wpart, wup, wdown, s)
-            if s < 4:
-                ring_send(wpart, wup, wdown, s + 1)
+            for h in range(2):
+                for side in range(2):
+                    wring_in(s, h, side).wait_recv()
+                if s < 3:
+                    for side in range(2):
+                        wring(s + 1, h, side).start()
             for d in tiles(s):
                 wpartner(d).start()
 
@@ -292,74 +298,79 @@
             ring_wait(hpart, hup, hdown, s)
             if s < 4:
                 ring_send(hpart, hup, hdown, s + 1)
-        x1_send(s)
 
     def wready(s):
         with jax.named_scope(f"wready{s}"):
             for d in tiles(s):
                 wpartner_in(d).wait_recv()
 
-    vert_peers(lambda q: w1(q).start())
+    def w1_wait(i):
+        with jax.named_scope(f"wtiles{i}"):
+            w1_all(i).wait_recv()
+            wpartner(4 * i).start()
+
+    vert_peers(lambda q: w1(0, q).start())
     ring_send(hpart, hup, hdown, 1)
     x1_send(0)
+    vert_peers(lambda q: w1(1, q).start())
     hstep(1)
-    with jax.named_scope("wtiles"):
-        w1_all().wait_recv()
-    ring_send(wpart, wup, wdown, 1)
-    wpartner(0).start()
+    x1_send(1)
+    w1_wait(0)
+    for h in range(2):
+        for side in range(2):
+            wring(1, h, side).start()
     loads[6].wait()
     wready(0)
     project(0)
+    w1_wait(1)
+    wstep(1)
     hstep(2)
-    x2_send(0)
-    x2_send(1)
-    wstep(1)
     wready(1)
     project(1)
-    hstep(3)
+    x1_send(2)
+    x2_send(0)
+    wstep(2)
     convolve(0)
-    wstep(2)
-    x2_send(2)
     wready(2)
     project(2)
-    hstep(4)
+    hstep(3)
+    x1_send(3)
     wstep(3)
+    convolve(1)
     wready(3)
     project(3)
-    x2_send(3)
-    convolve(1)
-    xdone(0)
-    xdone(1)
-    wstep(4)
     wready(4)
     project(4)
-    x2_send(4)
+    x2_send(1)
     convolve(2)
-    xdone(2)
+    hstep(4)
+    x1_send(4)
+    xdone(0)
     convolve(3)
-    xdone(3)
     convolve(4)
-    xdone(4)
-    with jax.named_scope("hready"):
-        for d in range(YS):
-            hpartner_in(d).wait_recv()
+    x2_send(2)
+    xdone(1)
     with jax.named_scope("gwait"):
         regroup_all().wait_recv()
 
-    def give(g, t):
-        return copy(att.at[g, :, t], ret.at[g, m], a_s.at[0], a_r.at[g], {"tm": t})
-
-    def give_all(g):
+    order = (0, 1, -1, 2, -2, 3, -3, 4)
+
+    def give(i, t):
+        return copy(att.at[i, :, t], ret.at[i, m], a_s.at[0], a_r.at[i], {"tm": t})
+
+    def give_all(i):
         most = pl.ds(0, TM - 1)
-        return copy(ret.at[g, most], ret.at[g, most], a_s.at[0], a_r.at[g], to_tm(1, c))
+        return copy(ret.at[i, most], ret.at[i, most], a_s.at[0], a_r.at[i], to_tm(1, c))
 
     def give_out():
         most = pl.ds(0, TM - 1)
         return copy(ret.at[:, most], ret.at[:, most], a_s.at[0], a_r.at[0], to_tm(1, c))
 
-    def attend(g):
-        with jax.named_scope("attend"):
-            wide = hwg[g].reshape(384, 1024)
+    def attend(i):
+        with jax.named_scope(f"hready{i}"):
+            hpartner_in(order[i]).wait_recv()
+        with jax.named_scope(f"attend{i}"):
+            wide = hwg[pos(order[i])].reshape(384, 1024)
             packed = None
             for ch in range(4):
                 seen = jnp.concatenate(
@@ -381,17 +392,30 @@
                     attention = (exponent * scale).astype(BF16)
                     outs.append(jnp.dot(value, attention, preferred_element_type=F32))
                 block = jnp.concatenate(outs, axis=0)
-                att[g, b] = block.T.astype(BF16).reshape(TM, 16, 128)
-            tm_peers(lambda t: give(g, t).start())
-            ret[g, m] = att[g, :, m]
-
-    loop(0, YS, attend)
+                att[i, b] = block.T.astype(BF16).reshape(TM, 16, 128)
+            tm_peers(lambda t: give(i, t).start())
+            ret[i, m] = att[i, :, m]
+
+    for i in range(YS):
+        attend(i)
+        if i == 0:
+            x2_send(3)
+            xdone(2)
+        if i == 1:
+            x2_send(4)
+        if i == 3:
+            xdone(3)
+        if i == 5:
+            xdone(4)
 
     with jax.named_scope("sent"):
-        w1_all().wait_send()
+        for i in range(2):
+            w1_all(i).wait_send()
         for s in range(1, 5):
-            up(wpart, wup, s).wait_send()
-            down(wpart, wdown, s).wait_send()
+            if s < 4:
+                for h in range(2):
+                    for side in range(2):
+                        wring(s, h, side).wait_send()
             up(hpart, hup, s).wait_send()
             down(hpart, hdown, s).wait_send()
         for d in range(YS):
@@ -404,13 +428,15 @@
             boundary_all(s).wait_send()
         regroup_all().wait_send()
 
-    def finish(g):
-        with jax.named_scope("await"):
-            give_all(g).wait_recv()
-        total = hid[g].reshape(512, 128).astype(F32) + ret[g].reshape(512, 128).astype(F32)
-        out[:, pl.ds(pl.multiple_of(g * 128, 128), 128)] = total.astype(BF16)
-
-    loop(0, YS, finish)
+    for i in range(YS):
+        with jax.named_scope(f"await{i}"):
+            give_all(i).wait_recv()
+        for yy in range(YS):
+            ct = (yy + order[i]) % YS
+            pair = pl.ds(2 * yy, 2)
+            total = (hid[ct, pair].reshape(64, 128).astype(F32)
+                     + ret[i, pair].reshape(64, 128).astype(F32))
+            out[yy * 64:(yy + 1) * 64, ct * 128:(ct + 1) * 128] = total.astype(BF16)
     with jax.named_scope("last"):
         give_out().wait_send()
 
@@ -446,8 +472,8 @@
             pltpu.VMEM((512, 512), BF16),
             pltpu.VMEM((512, 1024), BF16),
             pltpu.VMEM((256, 256), F32),
-            dma((7,)), dma((1,)), dma((1,)),
-            dma((5,)), dma((5,)), dma((5,)), dma((5,)), dma((YS,)), dma((YS,)),
+            dma((7,)), dma((2,)), dma((2,)),
+            dma((2, 4, 2)), dma((2, 4, 2)), dma((YS,)), dma((YS,)),
             dma((5,)), dma((5,)), dma((5,)), dma((5,)),
             dma((2, YS)), dma((2, YS)), dma((2, YS)), dma((2, YS)),
             dma((YS,)), dma((YS,)),

time: 101 us -> 91.7 us (0.908)
  Pallas kernels: 99.7 us -> 90.6 us
    pallas_call x1, Pallas kernels: 99.7 us -> 90.6 us  [layer(): pl.pallas_call(layer_kernel, out_shape=jax.ShapeDtypeStruct((512, 1024),...]
where the time goes in v3:
time: 91.7 us; the launch traced here: 91.6 us
  Pallas kernels  90.6 us (99%)
  local copies, waits for them, and re-layouts  0.97 us (1%)
    pallas_call x1, Pallas kernels, layer(): pl.pallas_call(layer_kernel, out_shape=jax.ShapeDtypeStruct((512, 1024),...  90.6 us

profile of v3, /device:TPU:1, one launch (start us, length us, event | category | flops | bytes accessed | tf_op | source)
XLA Modules:
  0.0 91.6 jit_solution(3274900149057487520)
XLA Ops:
  0.0 90.6 %shard_map.73 = bf16[512,1024]{1,0:T(8,128)(2,1)S(1)} custom-call(bf16[512,1024]{1,0:T(8,128)(2,1)} %bitcast.12, bf16[32,1024]{1,0:T(8,128)(2,1)} %weight_in.1, bf16[4,48,1024]{2,1,0:T(8,128)(2,1)} %bitcast.13, s32[16,32]{1,0:T(8,128)} %bitcast.15, s32[1,32]{1,0:T(1,128)} %bitcast.17, bf16[3,512,128]{2,1,0:T(8,128)(2,1)} %bitcast.14, s32[3,1,4]{2,1,0:T(1,128)} %bitcast.16), custom_call_target="tpu_custom_call" | custom-call | tf_op jit(solution)/shard_map/pallas_call | solution.py:448
  90.6 1.0 %copy.9 = bf16[1,512,1024]{2,1,0:T(8,128)(2,1)} copy(bf16[1,512,1024]{2,1,0:T(8,128)(2,1)S(1)} %bitcast.11) | data formatting | bytes 2097152

commit v4 on v3

--- a/solution.py
+++ b/solution.py
@@ -311,9 +311,9 @@
 
     vert_peers(lambda q: w1(0, q).start())
     ring_send(hpart, hup, hdown, 1)
+    hstep(1)
+    vert_peers(lambda q: w1(1, q).start())
     x1_send(0)
-    vert_peers(lambda q: w1(1, q).start())
-    hstep(1)
     x1_send(1)
     w1_wait(0)
     for h in range(2):
@@ -322,11 +322,11 @@
     loads[6].wait()
     wready(0)
     project(0)
-    w1_wait(1)
     wstep(1)
     hstep(2)
     wready(1)
     project(1)
+    w1_wait(1)
     x1_send(2)
     x2_send(0)
     wstep(2)
@@ -358,6 +358,9 @@
     def give(i, t):
         return copy(att.at[i, :, t], ret.at[i, m], a_s.at[0], a_r.at[i], {"tm": t})
 
+    def give_half(b, t):
+        return copy(att.at[0, b, t], ret.at[0, m, b], a_s.at[0], a_r.at[0], {"tm": t})
+
     def give_all(i):
         most = pl.ds(0, TM - 1)
         return copy(ret.at[i, most], ret.at[i, most], a_s.at[0], a_r.at[i], to_tm(1, c))
@@ -371,29 +374,35 @@
             hpartner_in(order[i]).wait_recv()
         with jax.named_scope(f"attend{i}"):
             wide = hwg[pos(order[i])].reshape(384, 1024)
-            packed = None
-            for ch in range(4):
-                seen = jnp.concatenate(
-                    [xg[2 * ch].reshape(512, 128), xg[2 * ch + 1].reshape(512, 128)], axis=1)
-                term = dot_last(wide[:, ch * WIDE:(ch + 1) * WIDE], seen)
-                packed = term if packed is None else packed + term
-            packed = packed.astype(BF16)
-            for b in range(2):
-                cols = slice(b * 256, (b + 1) * 256)
-                outs = []
-                for j in range(2):
-                    query = packed[192 * j:192 * j + 64, cols]
-                    key = packed[192 * j + 64:192 * j + 128, cols]
-                    value = packed[192 * j + 128:192 * j + 192, cols]
-                    score = dot_first(key, query) * 0.125 + bias[...]
-                    top = jnp.max(score, axis=0, keepdims=True)
-                    exponent = jnp.exp(score - top)
-                    scale = 1.0 / jnp.sum(exponent, axis=0, keepdims=True)
-                    attention = (exponent * scale).astype(BF16)
-                    outs.append(jnp.dot(value, attention, preferred_element_type=F32))
-                block = jnp.concatenate(outs, axis=0)
-                att[i, b] = block.T.astype(BF16).reshape(TM, 16, 128)
-            tm_peers(lambda t: give(i, t).start())
+            for part in ((0,), (1,)) if i == 0 else ((0, 1),):
+                count_rows = 256 * len(part)
+                packed = None
+                for ch in range(4):
+                    seen = jnp.concatenate(
+                        [xg[ct, part[0]:part[-1] + 1].reshape(count_rows, 128)
+                         for ct in (2 * ch, 2 * ch + 1)], axis=1)
+                    term = dot_last(wide[:, ch * WIDE:(ch + 1) * WIDE], seen)
+                    packed = term if packed is None else packed + term
+                packed = packed.astype(BF16)
+                for n, b in enumerate(part):
+                    cols = slice(n * 256, (n + 1) * 256)
+                    outs = []
+                    for j in range(2):
+                        query = packed[192 * j:192 * j + 64, cols]
+                        key = packed[192 * j + 64:192 * j + 128, cols]
+                        value = packed[192 * j + 128:192 * j + 192, cols]
+                        score = dot_first(key, query) * 0.125 + bias[...]
+                        top = jnp.max(score, axis=0, keepdims=True)
+                        exponent = jnp.exp(score - top)
+                        scale = 1.0 / jnp.sum(exponent, axis=0, keepdims=True)
+                        attention = (exponent * scale).astype(BF16)
+                        outs.append(jnp.dot(value, attention, preferred_element_type=F32))
+                    block = jnp.concatenate(outs, axis=0)
+                    att[i, b] = block.T.astype(BF16).reshape(TM, 16, 128)
+                    if i == 0:
+                        tm_peers(lambda t: give_half(b, t).start())
+            if i > 0:
+                tm_peers(lambda t: give(i, t).start())
             ret[i, m] = att[i, :, m]
 
     for i in range(YS):

time: 91.7 us -> 92 us (level)
  no operation moved by 1% of the time
where the time goes in v4:
time: 92 us; the launch traced here: 91.9 us
  Pallas kernels  90.9 us (99%)
  local copies, waits for them, and re-layouts  0.97 us (1%)
    pallas_call x1, Pallas kernels, layer(): pl.pallas_call(layer_kernel, out_shape=jax.ShapeDtypeStruct((512, 1024),...  90.9 us

profile of v4, /device:TPU:1, one launch (start us, length us, event | category | flops | bytes accessed | tf_op | source)
XLA Modules:
  0.0 91.9 jit_solution(10638406038184173851)
XLA Ops:
  0.0 90.9 %shard_map.73 = bf16[512,1024]{1,0:T(8,128)(2,1)S(1)} custom-call(bf16[512,1024]{1,0:T(8,128)(2,1)} %bitcast.12, bf16[32,1024]{1,0:T(8,128)(2,1)} %weight_in.1, bf16[4,48,1024]{2,1,0:T(8,128)(2,1)} %bitcast.13, s32[16,32]{1,0:T(8,128)} %bitcast.15, s32[1,32]{1,0:T(1,128)} %bitcast.17, bf16[3,512,128]{2,1,0:T(8,128)(2,1)} %bitcast.14, s32[3,1,4]{2,1,0:T(1,128)} %bitcast.16), custom_call_target="tpu_custom_call" | custom-call | tf_op jit(solution)/shard_map/pallas_call | solution.py:457
  90.9 1.0 %copy.9 = bf16[1,512,1024]{2,1,0:T(8,128)(2,1)} copy(bf16[1,512,1024]{2,1,0:T(8,128)(2,1)S(1)} %bitcast.11) | data formatting | bytes 2097152
